TPU v7x, 256 devices: a whole 4x4x8 slice. The times are simulated.
256 devices in a mesh: gx: 32 (over z, x_hi, core), gy: 8 (over y, x_lo).
Axes of the slice: x: 4 (x_hi: 2, x_lo: 2; x = x_hi * 2 + x_lo), y: 4, z: 8, core: 2. Of those that a mesh axis runs over, the one named last changes fastest.
Arguments:
- features: bfloat16 [32, 8, 3, 64, 256], P('gx', 'gy'), may hold values from -6 to 6
- block_coords: int32 [32, 8, 3], P('gx', 'gy'), may hold values from 0 to 31, as said below
- block_counts: int32 [32, 8], P('gx', 'gy'), may hold values from 2 to 3, as said below
- first_weight: bfloat16 [6912, 256], replicated, may hold values from -0.078125 to 0.078125
- second_weight: bfloat16 [6912, 256], replicated, may hold values from -0.078125 to 0.078125
- cotangent: bfloat16 [32, 8, 3, 64, 256], P('gx', 'gy'), may hold values from -6 to 6
Outputs:
- output_features: float32 [32, 8, 3, 64, 256], P('gx', 'gy')
- input_grad: float32 [32, 8, 3, 64, 256], P('gx', 'gy')
- first_weight_grad: float32 [6912, 256], P('gx', 'gy')
- second_weight_grad: float32 [6912, 256], P('gx', 'gy')
Inputs may be any that keep to these rules, and one draw needn't show every extreme that they name: `block_coords`: within a tile all 3 entries are distinct block positions, so slots at or past the tile's count name blocks that are not active. Slots 0 and 1 are always live and hold blocks of the lowest block layer in opposite corners of the tile's 2 x 2 block columns. `block_counts`: at least one tile holds 3 live slots in every draw.
All inputs are finite; a program needn't handle non-finite values.
Results may differ from a plain program's by a relative error of at most 0.0029.
Values may be sent and summed in bfloat16 or wider, within the bound.
A program may use at most 128 MiB of HBM per device.

v0:
```python
import math

import jax
import jax.numpy as jnp
from jax import lax
from jax.sharding import PartitionSpec as P

C = 256
SLAB_BLOCKS = 8
MAX_BLOCKS = 3


def extended(cells, sides, width):
    for axis, dim in sides:
        count = lax.axis_size(axis)
        ends = count - 1
        head = lax.slice_in_dim(cells, 0, width, axis=dim)
        tail = lax.slice_in_dim(cells, cells.shape[dim] - width, cells.shape[dim], axis=dim)
        cells = jnp.concatenate(
            [
                lax.ppermute(tail, axis, [(i, (i + 1) % count) for i in range(ends)]),
                cells,
                lax.ppermute(head, axis, [((i + 1) % count, i) for i in range(ends)]),
            ],
            axis=dim,
        )
    return cells


def dense_grid(field, slot_blocks, slot_live):
    positions = jnp.arange(4 * SLAB_BLOCKS, dtype=jnp.int32)
    placing = ((slot_blocks[:, None] == positions[None, :]) & slot_live[:, None]).astype(
        jnp.bfloat16
    )
    flat_field = field.reshape(MAX_BLOCKS, 64 * C)
    blocks = lax.dot_general(
        placing, flat_field, (((0,), (0,)), ((), ())), preferred_element_type=jnp.float32
    )
    blocks = blocks.astype(jnp.bfloat16).reshape(2, 2, SLAB_BLOCKS, 4, 4, 4, C)
    return blocks.transpose(0, 3, 1, 4, 2, 5, 6).reshape(8, 8, 4 * SLAB_BLOCKS, C)


def extend(grid):
    widened = extended(grid, (("gx", 0), ("gy", 1)), 1)
    return jnp.pad(widened, ((0, 0), (0, 0), (1, 1), (0, 0)))


def columns(padded, slot_blocks):
    chan_width = padded.shape[3]
    start_x = slot_blocks // (2 * SLAB_BLOCKS)
    start_y = slot_blocks // SLAB_BLOCKS % 2
    start_z = slot_blocks % SLAB_BLOCKS

    def cut_cube(block_x, block_y, block_z):
        return lax.dynamic_slice(
            padded, (4 * block_x, 4 * block_y, 4 * block_z, block_x * 0), (6, 6, 6, chan_width)
        )

    cubes = jax.vmap(cut_cube)(start_x, start_y, start_z)
    tap_list = []
    for tap_index in range(27):
        shift_x = tap_index // 9
        shift_y = tap_index // 3 % 3
        shift_z = tap_index % 3
        piece = cubes[:, shift_x : shift_x + 4, shift_y : shift_y + 4, shift_z : shift_z + 4, :]
        tap_list.append(piece.reshape(-1, chan_width))
    return jnp.concatenate(tap_list, axis=1)


def transposed(cols, weight):
    chan_width = weight.shape[1]
    stacked = cols.reshape(cols.shape[0], 27, chan_width)
    flipped = weight.reshape(27, chan_width, chan_width)[::-1]
    return lax.dot_general(
        stacked, flipped, (((1, 2), (0, 2)), ((), ())), preferred_element_type=jnp.float32
    )


def contract_rows(cols, rows):
    return lax.dot_general(cols, rows, (((0,), (0,)), ((), ())), preferred_element_type=jnp.float32)


def reduce_weights(term):
    narrowed = lax.psum_scatter(term, "gx", scatter_dimension=0, tiled=True)
    return lax.psum_scatter(narrowed, "gy", scatter_dimension=1, tiled=True)


def per_device(features, block_coords, block_counts, first_weight, second_weight, cotangent):
    slot_blocks = block_coords.reshape(MAX_BLOCKS)
    slot_live = jnp.arange(MAX_BLOCKS, dtype=jnp.int32) < block_counts.reshape(())
    row_live = jnp.repeat(slot_live, 64)[:, None]
    zero_float = jnp.zeros((), jnp.float32)
    feature_cols = columns(extend(dense_grid(features, slot_blocks, slot_live)), slot_blocks)
    pre_first = jnp.dot(feature_cols, first_weight, preferred_element_type=jnp.float32)
    hidden = jnp.where(row_live, jax.nn.silu(pre_first), zero_float).astype(jnp.bfloat16)
    hidden_cols = columns(extend(dense_grid(hidden, slot_blocks, slot_live)), slot_blocks)
    output_rows = jnp.where(
        row_live,
        jnp.dot(hidden_cols, second_weight, preferred_element_type=jnp.float32),
        zero_float,
    )
    seed_rows = jnp.where(row_live, cotangent.reshape(-1, C), jnp.zeros((), jnp.bfloat16))
    seed_cols = columns(extend(dense_grid(cotangent, slot_blocks, slot_live)), slot_blocks)
    grad_scale = 1.0 / math.sqrt(64 * MAX_BLOCKS * lax.axis_size("gx") * lax.axis_size("gy"))
    second_term = contract_rows(hidden_cols, seed_rows) * grad_scale
    hidden_grad = transposed(seed_cols, second_weight)
    sigmoid_pre = jax.nn.sigmoid(pre_first)
    pre_grad = jnp.where(
        row_live, hidden_grad * sigmoid_pre * (1.0 + pre_first * (1.0 - sigmoid_pre)), zero_float
    ).astype(jnp.bfloat16)
    grad_cols = columns(extend(dense_grid(pre_grad, slot_blocks, slot_live)), slot_blocks)
    first_term = contract_rows(feature_cols, pre_grad) * grad_scale
    first_grad = reduce_weights(first_term)
    input_rows = jnp.where(row_live, transposed(grad_cols, first_weight), zero_float)
    second_grad = reduce_weights(second_term)
    return (
        output_rows.reshape(features.shape),
        input_rows.reshape(features.shape),
        first_grad,
        second_grad,
    )


def solution(mesh):
    placed = (
        P("gx", "gy", None, None, None),
        P("gx", "gy", None),
        P("gx", "gy"),
        P(),
        P(),
        P("gx", "gy", None, None, None),
    )
    return jax.shard_map(
        per_device,
        mesh=mesh,
        in_specs=placed,
        out_specs=(
            P("gx", "gy", None, None, None),
            P("gx", "gy", None, None, None),
            P("gx", "gy"),
            P("gx", "gy"),
        ),
        check_vma=False,
    )
```

profile of v0, /device:TPU:32, one launch (start us, length us, event | category | flops | bytes accessed | tf_op | source)
XLA Modules:
  0.0 612.2 jit_solution(4846355329869789446)
XLA Ops:
  17.8 6.0 collective-permute-start.9
  32.7 6.0 collective-permute-start.1
  52.7 5.2 collective-permute-start.2
  62.7 12.6 %while.6 = (s32[]{:T(128)}, bf16[10,10,34,256]{3,2,1,0:T(8,128)(2,1)}, s32[3,4]{1,0:T(4,128)S(1)}, bf16[3,6,6,6,256]{4,3,2,1,0:T(8,128)(2,1)}, s32[]{:T(128)}) while((s32[]{:T(128)}, bf16[10,10,34,256]{3,2,1,0:T(8,128)(2,1)}, s32[3,4]{1,0:T(4,128)S(1)}, bf16[3,6,6,6,256]{4,3,2,1,0:T(8,128)(2,1)}, s32[]{:T(128)}) %tuple.196), condition=%wide.while_cond.2, body=%wide.while_body.2.sunk | while | flops 2 | bytes 297081 | solution.py:55
  75.3 5.3 fusion.29
  86.2 12.6 %while.4 = (s32[]{:T(128)}, bf16[10,10,34,256]{3,2,1,0:T(8,128)(2,1)}, s32[3,4]{1,0:T(4,128)S(1)}, bf16[3,6,6,6,256]{4,3,2,1,0:T(8,128)(2,1)}, s32[]{:T(128)}) while((s32[]{:T(128)}, bf16[10,10,34,256]{3,2,1,0:T(8,128)(2,1)}, s32[3,4]{1,0:T(4,128)S(1)}, bf16[3,6,6,6,256]{4,3,2,1,0:T(8,128)(2,1)}, s32[]{:T(128)}) %tuple.210), condition=%wide.while_cond, body=%wide.while_body.sunk | while | flops 2 | bytes 297081 | solution.py:55
  231.3 4.0 convolution_multiply_fusion.1
  246.1 6.2 %collective-permute-start.5 = (bf16[1,8,32,256]{3,2,1,0:T(8,128)(2,1)}, bf16[1,8,32,256]{3,2,1,0:T(8,128)(2,1)S(1)}, u32[]{:S(2)}, u32[]{:S(2)}) collective-permute-start(bf16[1,8,32,256]{3,2,1,0:T(8,128)(2,1)} %get-tuple-element.132), channel_id=1, source_target_pairs={{8,0},{16,8},{24,16},{32,24},{40,32},{48,40},{56,48},{64,56},{72,6... | collective-permute-start | bytes 393224 | tf_op jit(solution)/shard_map/ppermute | solution.py:23
  255.5 4.6 collective-permute-start.6
  262.9 7.5 %collective-permute-done.7 = bf16[10,1,32,256]{3,2,1,0:T(8,128)(2,1)S(1)} collective-permute-done((bf16[10,1,32,256]{3,2,1,0:T(8,128)(2,1)S(1)}, bf16[10,1,32,256]{3,2,1,0:T(8,128)(2,1)S(1)}, u32[]{:S(2)}, u32[]{:S(2)}) %collective-permute-start.7) | collective-permute-done | bytes 163872 | tf_op jit(solution)/shard_map/ppermute | solution.py:23
  273.7 12.6 %while.5 = (s32[]{:T(128)}, bf16[10,10,34,256]{3,2,1,0:T(8,128)(2,1)}, s32[3,4]{1,0:T(4,128)S(1)}, bf16[3,6,6,6,256]{4,3,2,1,0:T(8,128)(2,1)}, s32[]{:T(128)}) while((s32[]{:T(128)}, bf16[10,10,34,256]{3,2,1,0:T(8,128)(2,1)}, s32[3,4]{1,0:T(4,128)S(1)}, bf16[3,6,6,6,256]{4,3,2,1,0:T(8,128)(2,1)}, s32[]{:T(128)}) %tuple.211), condition=%wide.while_cond.1, body=%wide.while_body.1.sunk | while | flops 2 | bytes 297081 | solution.py:55
  301.8 5.4 fusion.31
  351.5 4.1 convolution_multiply_fusion
  365.3 6.0 collective-permute-start.13
  380.6 5.5 collective-permute-done.15
  389.5 12.7 %while.7 = (s32[]{:T(128)}, bf16[10,10,34,256]{3,2,1,0:T(8,128)(2,1)}, s32[3,4]{1,0:T(4,128)S(1)}, bf16[3,6,6,6,256]{4,3,2,1,0:T(8,128)(2,1)}, s32[]{:T(128)}) while((s32[]{:T(128)}, bf16[10,10,34,256]{3,2,1,0:T(8,128)(2,1)}, s32[3,4]{1,0:T(4,128)S(1)}, bf16[3,6,6,6,256]{4,3,2,1,0:T(8,128)(2,1)}, s32[]{:T(128)}) %tuple.212), condition=%wide.while_cond.3, body=%wide.while_body.3.sunk | while | flops 2 | bytes 297081 | solution.py:55
  390.1 3.6 bitcast_dynamic-update-slice_fusion.11
  394.3 3.7 bitcast_dynamic-update-slice_fusion.11
  417.6 5.3 fusion.27
  484.9 4.3 convolution_select_fusion
  489.2 33.2 %reduce-scatter.11.cloned.1.call-done = f32[216,256]{1,0:T(8,128)} async-done(((f32[6912,256]{1,0:T(8,128)}), f32[216,256]{1,0:T(8,128)}) %reduce-scatter.11.cloned.1.call-update) | async-done | bytes 221200 | tf_op jit(solution)/shard_map/reduce_scatter | solution.py:84
  525.8 3.7 fusion.9
  529.5 34.5 %reduce-scatter.13.cloned.1.call-done = f32[32,216]{1,0:T(8,128)} async-done(((f32[256,216]{1,0:T(8,128)}), f32[32,216]{1,0:T(8,128)}) %reduce-scatter.13.cloned.1.call-update) | async-done | bytes 27664
  564.0 41.7 %reduce-scatter.15.cloned.1.call-done = f32[32,216]{1,0:T(8,128)} async-done(((f32[256,216]{1,0:T(8,128)}), f32[32,216]{1,0:T(8,128)}) %reduce-scatter.15.cloned.1.call-update) | async-done | bytes 27664
  (489 shorter events, 400.3 us)
Async XLA Ops:
  7.2 219.3 %copy-start = (bf16[6912,256]{1,0:T(8,128)(2,1)S(1)}, bf16[6912,256]{1,0:T(8,128)(2,1)}, u32[]{:S(2)}) copy-start(bf16[6912,256]{1,0:T(8,128)(2,1)} %param.9) | copy-start | bytes 10616836
  7.2 472.8 %reduce-scatter.9.cloned.1.call-start = ((), (), s32[]{:S(2)}) async-start(), calls=%async_computation.4 | async-start | bytes 7299072 | tf_op jit(solution)/shard_map/reduce_scatter | solution.py:84
  15.9 25.0 %collective-permute-start.8 = (bf16[1,8,32,256]{3,2,1,0:T(8,128)(2,1)}, bf16[1,8,32,256]{3,2,1,0:T(8,128)(2,1)}, u32[]{:S(2)}, u32[]{:S(2)}) collective-permute-start(bf16[1,8,32,256]{3,2,1,0:T(8,128)(2,1)} %get-tuple-element.131), channel_id=1, source_target_pairs={{0,8},{8,16},{16,24},{24,32},{32,40},{40,48},{48,56},{56,64},{64,7... | collective-permute-start | bytes 393224 | tf_op jit(solution)/shard_map/ppermute | solution.py:21
  17.8 25.4 %collective-permute-start.9 = (bf16[1,8,32,256]{3,2,1,0:T(8,128)(2,1)}, bf16[1,8,32,256]{3,2,1,0:T(8,128)(2,1)}, u32[]{:S(2)}, u32[]{:S(2)}) collective-permute-start(bf16[1,8,32,256]{3,2,1,0:T(8,128)(2,1)} %get-tuple-element.130), channel_id=1, source_target_pairs={{8,0},{16,8},{24,16},{32,24},{40,32},{48,40},{56,48},{64,56},{72,6... | collective-permute-start | bytes 393224 | tf_op jit(solution)/shard_map/ppermute | solution.py:23
  30.7 18.2 %collective-permute-start = (bf16[1,8,32,256]{3,2,1,0:T(8,128)(2,1)}, bf16[1,8,32,256]{3,2,1,0:T(8,128)(2,1)}, u32[]{:S(2)}, u32[]{:S(2)}) collective-permute-start(bf16[1,8,32,256]{3,2,1,0:T(8,128)(2,1)} %get-tuple-element.135), channel_id=1, source_target_pairs={{0,8},{8,16},{16,24},{24,32},{32,40},{40,48},{48,56},{56,64},{64,7... | collective-permute-start | bytes 393224 | tf_op jit(solution)/shard_map/ppermute | solution.py:21
  32.7 17.3 %collective-permute-start.1 = (bf16[1,8,32,256]{3,2,1,0:T(8,128)(2,1)}, bf16[1,8,32,256]{3,2,1,0:T(8,128)(2,1)}, u32[]{:S(2)}, u32[]{:S(2)}) collective-permute-start(bf16[1,8,32,256]{3,2,1,0:T(8,128)(2,1)} %get-tuple-element.134), channel_id=1, source_target_pairs={{8,0},{16,8},{24,16},{32,24},{40,32},{48,40},{56,48},{64,56},{72,6... | collective-permute-start | bytes 393224 | tf_op jit(solution)/shard_map/ppermute | solution.py:23
  44.2 15.2 %collective-permute-start.10 = (bf16[10,1,32,256]{3,2,1,0:T(8,128)(2,1)S(1)}, bf16[10,1,32,256]{3,2,1,0:T(8,128)(2,1)S(1)}, u32[]{:S(2)}, u32[]{:S(2)}) collective-permute-start(bf16[10,1,32,256]{3,2,1,0:T(8,128)(2,1)S(1)} %get-tuple-element.122), channel_id=1, source_target_pairs={{0,1},{1,2},{2,3},{3,4},{4,5},{5,6},{6,7},{8,9},{9,10},{10,11},{11... | collective-permute-start | bytes 491528 | tf_op jit(solution)/shard_map/ppermute | solution.py:21
  47.6 11.8 %collective-permute-start.11 = (bf16[10,1,32,256]{3,2,1,0:T(8,128)(2,1)S(1)}, bf16[10,1,32,256]{3,2,1,0:T(8,128)(2,1)S(1)}, u32[]{:S(2)}, u32[]{:S(2)}) collective-permute-start(bf16[10,1,32,256]{3,2,1,0:T(8,128)(2,1)S(1)} %get-tuple-element.123), channel_id=1, source_target_pairs={{1,0},{2,1},{3,2},{4,3},{5,4},{6,5},{7,6},{9,8},{10,9},{11,10},{12... | collective-permute-start | bytes 491528 | tf_op jit(solution)/shard_map/ppermute | solution.py:23
  52.7 29.2 %collective-permute-start.2 = (bf16[10,1,32,256]{3,2,1,0:T(8,128)(2,1)}, bf16[10,1,32,256]{3,2,1,0:T(8,128)(2,1)}, u32[]{:S(2)}, u32[]{:S(2)}) collective-permute-start(bf16[10,1,32,256]{3,2,1,0:T(8,128)(2,1)} %get-tuple-element.126), channel_id=1, source_target_pairs={{0,1},{1,2},{2,3},{3,4},{4,5},{5,6},{6,7},{8,9},{9,10},{10,11},{11... | collective-permute-start | bytes 491528 | tf_op jit(solution)/shard_map/ppermute | solution.py:21
  57.9 24.0 %collective-permute-start.3 = (bf16[10,1,32,256]{3,2,1,0:T(8,128)(2,1)}, bf16[10,1,32,256]{3,2,1,0:T(8,128)(2,1)}, u32[]{:S(2)}, u32[]{:S(2)}) collective-permute-start(bf16[10,1,32,256]{3,2,1,0:T(8,128)(2,1)} %get-tuple-element.127), channel_id=1, source_target_pairs={{1,0},{2,1},{3,2},{4,3},{5,4},{6,5},{7,6},{9,8},{10,9},{11,10},{12... | collective-permute-start | bytes 491528 | tf_op jit(solution)/shard_map/ppermute | solution.py:23
  191.1 34.7 %copy-start.5 = (bf16[192,6912]{1,0:T(8,128)(2,1)S(1)}, bf16[192,6912]{1,0:T(8,128)(2,1)}, u32[]{:S(2)}) copy-start(bf16[192,6912]{1,0:T(8,128)(2,1)} %constant_dynamic-update-slice_fusion.29) | copy-start | bytes 7962628
  191.1 34.7 %copy-start.40 = (bf16[192,256]{1,0:T(8,128)(2,1)S(1)}, bf16[192,256]{1,0:T(8,128)(2,1)}, u32[]{:S(2)}) copy-start(bf16[192,256]{1,0:T(8,128)(2,1)} %reshape.617) | copy-start | bytes 294916
  191.1 34.7 %copy-start.41 = (bf16[192,256]{1,0:T(8,128)(2,1)S(1)}, bf16[192,256]{1,0:T(8,128)(2,1)}, u32[]{:S(2)}) copy-start(bf16[192,256]{1,0:T(8,128)(2,1)} %reshape.618) | copy-start | bytes 294916
  235.4 287.0 %reduce-scatter.11.cloned.1.call-start = ((), (), s32[]{:S(2)}) async-start(), calls=%async_computation.5 | async-start | bytes 7299072 | tf_op jit(solution)/shard_map/reduce_scatter | solution.py:84
  244.1 9.0 %collective-permute-start.4 = (bf16[1,8,32,256]{3,2,1,0:T(8,128)(2,1)}, bf16[1,8,32,256]{3,2,1,0:T(8,128)(2,1)}, u32[]{:S(2)}, u32[]{:S(2)}) collective-permute-start(bf16[1,8,32,256]{3,2,1,0:T(8,128)(2,1)} %get-tuple-element.133), channel_id=1, source_target_pairs={{0,8},{8,16},{16,24},{24,32},{32,40},{40,48},{48,56},{56,64},{64,7... | collective-permute-start | bytes 393224 | tf_op jit(solution)/shard_map/ppermute | solution.py:21
  246.1 9.4 %collective-permute-start.5 = (bf16[1,8,32,256]{3,2,1,0:T(8,128)(2,1)}, bf16[1,8,32,256]{3,2,1,0:T(8,128)(2,1)S(1)}, u32[]{:S(2)}, u32[]{:S(2)}) collective-permute-start(bf16[1,8,32,256]{3,2,1,0:T(8,128)(2,1)} %get-tuple-element.132), channel_id=1, source_target_pairs={{8,0},{16,8},{24,16},{32,24},{40,32},{48,40},{56,48},{64,56},{72,6... | collective-permute-start | bytes 393224 | tf_op jit(solution)/shard_map/ppermute | solution.py:23
  255.5 7.4 %collective-permute-start.6 = (bf16[10,1,32,256]{3,2,1,0:T(8,128)(2,1)S(1)}, bf16[10,1,32,256]{3,2,1,0:T(8,128)(2,1)S(1)}, u32[]{:S(2)}, u32[]{:S(2)}) collective-permute-start(bf16[10,1,32,256]{3,2,1,0:T(8,128)(2,1)S(1)} %get-tuple-element.124), channel_id=1, source_target_pairs={{0,1},{1,2},{2,3},{3,4},{4,5},{5,6},{6,7},{8,9},{9,10},{10,11},{11... | collective-permute-start | bytes 491528 | tf_op jit(solution)/shard_map/ppermute | solution.py:21
  260.1 10.3 %collective-permute-start.7 = (bf16[10,1,32,256]{3,2,1,0:T(8,128)(2,1)S(1)}, bf16[10,1,32,256]{3,2,1,0:T(8,128)(2,1)S(1)}, u32[]{:S(2)}, u32[]{:S(2)}) collective-permute-start(bf16[10,1,32,256]{3,2,1,0:T(8,128)(2,1)S(1)} %get-tuple-element.125), channel_id=1, source_target_pairs={{1,0},{2,1},{3,2},{4,3},{5,4},{6,5},{7,6},{9,8},{10,9},{11,10},{12... | collective-permute-start | bytes 491528 | tf_op jit(solution)/shard_map/ppermute | solution.py:23
  355.6 208.4 %reduce-scatter.13.cloned.1.call-start = ((), (), s32[]{:S(2)}) async-start(), calls=%async_computation.6 | async-start | bytes 294912
  363.4 9.7 %collective-permute-start.12 = (bf16[1,8,32,256]{3,2,1,0:T(8,128)(2,1)S(1)}, bf16[1,8,32,256]{3,2,1,0:T(8,128)(2,1)S(1)}, u32[]{:S(2)}, u32[]{:S(2)}) collective-permute-start(bf16[1,8,32,256]{3,2,1,0:T(8,128)(2,1)S(1)} %get-tuple-element.129), channel_id=1, source_target_pairs={{0,8},{8,16},{16,24},{24,32},{32,40},{40,48},{48,56},{56,64},{64,7... | collective-permute-start | bytes 393224 | tf_op jit(solution)/shard_map/ppermute | solution.py:21
  365.3 9.2 %collective-permute-start.13 = (bf16[1,8,32,256]{3,2,1,0:T(8,128)(2,1)S(1)}, bf16[1,8,32,256]{3,2,1,0:T(8,128)(2,1)S(1)}, u32[]{:S(2)}, u32[]{:S(2)}) collective-permute-start(bf16[1,8,32,256]{3,2,1,0:T(8,128)(2,1)S(1)} %get-tuple-element.128), channel_id=1, source_target_pairs={{8,0},{16,8},{24,16},{32,24},{40,32},{48,40},{56,48},{64,56},{72,6... | collective-permute-start | bytes 393224 | tf_op jit(solution)/shard_map/ppermute | solution.py:23
  374.5 6.1 %collective-permute-start.14 = (bf16[10,1,32,256]{3,2,1,0:T(8,128)(2,1)S(1)}, bf16[10,1,32,256]{3,2,1,0:T(8,128)(2,1)S(1)}, u32[]{:S(2)}, u32[]{:S(2)}) collective-permute-start(bf16[10,1,32,256]{3,2,1,0:T(8,128)(2,1)S(1)} %get-tuple-element.120), channel_id=1, source_target_pairs={{0,1},{1,2},{2,3},{3,4},{4,5},{5,6},{6,7},{8,9},{9,10},{10,11},{11... | collective-permute-start | bytes 491528 | tf_op jit(solution)/shard_map/ppermute | solution.py:21
  377.3 8.8 %collective-permute-start.15 = (bf16[10,1,32,256]{3,2,1,0:T(8,128)(2,1)S(1)}, bf16[10,1,32,256]{3,2,1,0:T(8,128)(2,1)S(1)}, u32[]{:S(2)}, u32[]{:S(2)}) collective-permute-start(bf16[10,1,32,256]{3,2,1,0:T(8,128)(2,1)S(1)} %get-tuple-element.121), channel_id=1, source_target_pairs={{1,0},{2,1},{3,2},{4,3},{5,4},{6,5},{7,6},{9,8},{10,9},{11,10},{12... | collective-permute-start | bytes 491528 | tf_op jit(solution)/shard_map/ppermute | solution.py:23
  481.7 123.9 %reduce-scatter.15.cloned.1.call-start = ((), (), s32[]{:S(2)}) async-start(), calls=%async_computation.7 | async-start | bytes 294912
  (68 other events, 1123.6 us)
Sparse Core Ops, SparseCore 0:
  235.5 144.2 reduce-scatter.8
  384.2 138.1 reduce-scatter.10
  525.5 38.4 reduce-scatter.12
  567.0 38.5 reduce-scatter.14
where the time goes:
time: 619 us; the launch traced here: 612 us
  local copies, waits for them, and re-layouts  378 us (61%)
  waiting for transfers between devices  128 us (21%)
  starting transfers between devices  53.9 us (9%)
  matrix products  22.9 us (4%)
  between operations  15.9 us (3%)
  other arithmetic  13.7 us (2%)
    unnamed x265, local copies, waits for them, and re-layouts  101 us
    concatenate x58, local copies, waits for them, and re-layouts, columns(): return jnp.concatenate(tap_list, axis=1)  86.6 us
    reshape x54, local copies, waits for them, and re-layouts, columns(): tap_list.append(piece.reshape(-1, chan_width))  84.2 us
    unnamed x6, waiting for transfers between devices  76.2 us
    gather x36, local copies, waits for them, and re-layouts  50.6 us
    reduce_scatter x2, waiting for transfers between devices, reduce_weights(): narrowed = lax.psum_scatter(term, 'gx', scatter_dimension=0, tiled=True)  33.2 us
    ppermute x8, starting transfers between devices, extended(): lax.ppermute(head, axis, [((i + 1) % count, i) for i in range(ends)])  29.9 us
    slice x8, local copies, waits for them, and re-layouts, columns(): cubes[:, shift_x:shift_x + 4, shift_y:shift_y + 4, shift_z:shift_z + 4, :]  27.8 us
  transfers between devices with their start and end apart: 20, of which 9 were waited for; matrix products, arithmetic and copies ran while one was open for 41% of the time, Pallas kernels for 0%

commit v1 on v0

v1 whole, which is shorter than its diff:
```python
import functools
import math

import jax
import jax.numpy as jnp
import numpy as np
from jax import lax
from jax.experimental import pallas as pl
from jax.experimental.pallas import tpu as pltpu
from jax.sharding import PartitionSpec as P

C = 256
SLOTS = 3
ROWS = 192
FACE = 256
DATA = FACE + ROWS
DEAD = -(1 << 24)
MESH = pl.DeviceIdType.MESH
F32 = jnp.float32
BF16 = jnp.bfloat16

REGIONS = (
    (-1, 0, 0, 48),
    (1, 0, 48, 48),
    (0, -1, 96, 48),
    (0, 1, 144, 48),
    (-1, -1, 192, 16),
    (-1, 1, 208, 16),
    (1, -1, 224, 16),
    (1, 1, 240, 16),
)


def face_tables():
    source = np.full(FACE, -1, np.int64)
    table = np.zeros((8, FACE), np.int32)
    table[1] = DEAD
    for sx, sy, start, _ in REGIONS:
        xs = range(4) if sx == 0 else ((3,) if sx < 0 else (0,))
        ys = range(4) if sy == 0 else ((3,) if sy < 0 else (0,))
        row = start
        for slot in range(SLOTS):
            for vx in xs:
                for vy in ys:
                    for vz in range(4):
                        source[row] = slot * 64 + vx * 16 + vy * 4 + vz
                        table[0, row] = slot
                        table[1, row] = (
                            (8 * sx + vx + 1) * 4096 + (8 * sy + vy + 1) * 64 + vz + 1
                        )
                        row += 1
        table[2, start : start + (48 if sx * sy == 0 else 16)] = -sx
        table[3, start : start + (48 if sx * sy == 0 else 16)] = -sy
    for index, (_, _, start, count) in enumerate(REGIONS):
        table[4, start : start + count] = index
    pick = (source[:, None] == np.arange(ROWS)[None, :]).astype(np.float32)
    return pick, table


def block_codes(coords_ref, counts_ref):
    codes = []
    for slot in range(SLOTS):
        p = coords_ref[0, slot]
        code = (p // 16) * (4 * 4096) + ((p // 8) % 2) * (4 * 64) + (p % 8) * 4
        codes.append((code, slot < counts_ref[0, 0]))
    return codes


def by_slot(slot, codes):
    values = [jnp.where(live, code, DEAD) for code, live in codes]
    return jnp.where(slot == 0, values[0], jnp.where(slot == 1, values[1], values[2]))


def swap_faces(packed, landed, send_sems, recv_sems, extra=()):
    nx, ny = lax.axis_size("gx"), lax.axis_size("gy")
    gx, gy = lax.axis_index("gx"), lax.axis_index("gy")
    copies = []
    for index, (sx, sy, start, count) in enumerate(REGIONS):
        peer = (lax.rem(gx - sx + nx, nx), lax.rem(gy - sy + ny, ny))
        copies.append(
            pltpu.make_async_remote_copy(
                src_ref=packed.at[:, pl.ds(start, count), :],
                dst_ref=landed.at[:, pl.ds(start, count), :],
                send_sem=send_sems.at[index],
                recv_sem=recv_sems.at[index],
                device_id=peer,
                device_id_type=MESH,
            )
        )
        for source, target, sends, recvs in extra:
            copies.append(
                pltpu.make_async_remote_copy(
                    src_ref=source,
                    dst_ref=target.at[index],
                    send_sem=sends.at[index],
                    recv_sem=recvs.at[index],
                    device_id=peer,
                    device_id_type=MESH,
                )
            )
    return copies


def greet_around():
    nx, ny = lax.axis_size("gx"), lax.axis_size("gy")
    gx, gy = lax.axis_index("gx"), lax.axis_index("gy")
    barrier = pltpu.get_barrier_semaphore()
    for sx, sy, _, _ in REGIONS:
        peer = (lax.rem(gx - sx + nx, nx), lax.rem(gy - sy + ny, ny))
        pl.semaphore_signal(barrier, inc=1, device_id=peer, device_id_type=MESH)
    pl.semaphore_wait(barrier, 8)


def first_swap_kernel(
    feat_ref,
    cot_ref,
    pick_ref,
    table_ref,
    coords_ref,
    counts_ref,
    landed_out,
    code_out,
    packed,
    code,
    landed,
    codes_in,
    send_sems,
    recv_sems,
    code_send,
    code_recv,
):
    nx, ny = lax.axis_size("gx"), lax.axis_size("gy")
    gx, gy = lax.axis_index("gx"), lax.axis_index("gy")
    pick = pick_ref[...]
    packed[0] = jnp.dot(pick, feat_ref[...], preferred_element_type=F32).astype(BF16)
    packed[1] = jnp.dot(pick, cot_ref[...], preferred_element_type=F32).astype(BF16)
    blocks = block_codes(coords_ref, counts_ref)
    to_x = gx + table_ref[2:3, :]
    to_y = gy + table_ref[3:4, :]
    inside = (to_x >= 0) & (to_x < nx) & (to_y >= 0) & (to_y < ny)
    sent = table_ref[1:2, :] + by_slot(table_ref[0:1, :], blocks)
    code[...] = jnp.broadcast_to(jnp.where(inside, sent, DEAD), (8, FACE))
    greet_around()
    copies = swap_faces(
        packed, landed, send_sems, recv_sems, ((code, codes_in, code_send, code_recv),)
    )
    for copy in copies:
        copy.start()
    lane = lax.broadcasted_iota(jnp.int32, (8, ROWS), 1)
    voxel = lane % 64
    own = (voxel // 16 + 1) * 4096 + ((voxel // 4) % 4 + 1) * 64 + voxel % 4 + 1
    code_out[:, FACE:] = own + by_slot(lane // 64, blocks)
    for copy in copies:
        copy.wait()
    landed_out[...] = landed[...]
    region = jnp.broadcast_to(table_ref[4:5, :], (8, FACE))
    got = codes_in[0]
    for index in range(1, 8):
        got = jnp.where(region == index, codes_in[index], got)
    code_out[:, :FACE] = got


def second_swap_kernel(packed, landed_out, landed, send_sems, recv_sems):
    greet_around()
    copies = swap_faces(packed, landed, send_sems, recv_sems)
    for copy in copies:
        copy.start()
    for copy in copies:
        copy.wait()
    landed_out[...] = landed[...]


def build_windows(first, second, code_ref, coords_ref, win_ref):
    row = lax.broadcasted_iota(jnp.int32, (96, DATA), 0)
    pattern = (row // 16) * 4096 + ((row // 4) % 4) * 64 + row % 4
    offset = jnp.broadcast_to(code_ref[0:1, :], (96, DATA)) - pattern
    both = jnp.concatenate([first, second], axis=1)
    starts = []
    for slot in range(SLOTS):
        p = coords_ref[0, slot]
        starts.append((p // 16) * (4 * 4096) + ((p // 8) % 2) * (4 * 64) + (p % 8) * 4)
    for shift in range(9):
        placing = jnp.concatenate(
            [
                jnp.where(
                    offset == starts[slot] + (shift // 3) * 64 + shift % 3, 1.0, 0.0
                ).astype(BF16)
                for slot in range(SLOTS)
            ],
            axis=0,
        )
        rows = jnp.dot(placing, both, preferred_element_type=F32).astype(BF16)
        win_ref[0, shift] = rows[:, :C].reshape(SLOTS, 6, 16, C)
        win_ref[1, shift] = rows[:, C:].reshape(SLOTS, 6, 16, C)


def tap_rows(win_ref, field, tap):
    return win_ref[field, tap % 9, :, tap // 9 : tap // 9 + 4].reshape(ROWS, C)


def conv(win_ref, field, weight_ref):
    total = jnp.zeros((ROWS, C), F32)
    for tap in range(27):
        total += jnp.dot(
            tap_rows(win_ref, field, tap),
            weight_ref[tap * C : (tap + 1) * C, :],
            preferred_element_type=F32,
        )
    return total


def conv_back(win_ref, field, weight_ref):
    total = jnp.zeros((ROWS, C), F32)
    for tap in range(27):
        total += lax.dot_general(
            tap_rows(win_ref, field, 26 - tap),
            weight_ref[tap * C : (tap + 1) * C, :],
            (((1,), (1,)), ((), ())),
            preferred_element_type=F32,
        )
    return total


def live_rows(counts_ref):
    return lax.broadcasted_iota(jnp.int32, (ROWS, C), 0) < counts_ref[0, 0] * 64


def middle_kernel(
    feat_ref,
    cot_ref,
    landed_ref,
    code_ref,
    pick_ref,
    coords_ref,
    counts_ref,
    w1_hbm,
    w2_hbm,
    rows_out,
    packed_out,
    seed_win_out,
    win,
    w1,
    w2,
    sems,
):
    loads = [
        pltpu.make_async_copy(w1_hbm, w1, sems.at[0]),
        pltpu.make_async_copy(w2_hbm, w2, sems.at[1]),
    ]
    for load in loads:
        load.start()
    build_windows(
        jnp.concatenate([landed_ref[0], feat_ref[...]], axis=0),
        jnp.concatenate([landed_ref[1], cot_ref[...]], axis=0),
        code_ref,
        coords_ref,
        win,
    )
    live = live_rows(counts_ref)
    loads[0].wait()
    pre = conv(win, 0, w1)
    gate = jax.nn.sigmoid(pre)
    hidden = jnp.where(live, pre * gate, 0.0).astype(BF16)
    loads[1].wait()
    hidden_grad = conv_back(win, 1, w2)
    pre_grad = jnp.where(live, hidden_grad * gate * (1.0 + pre * (1.0 - gate)), 0.0).astype(BF16)
    rows_out[0] = hidden
    rows_out[1] = pre_grad
    pick = pick_ref[...]
    packed_out[0] = jnp.dot(pick, hidden, preferred_element_type=F32).astype(BF16)
    packed_out[1] = jnp.dot(pick, pre_grad, preferred_element_type=F32).astype(BF16)
    seed_win_out[...] = win[1]


def last_kernel(
    scale,
    rows_ref,
    landed_ref,
    code_ref,
    feat_ref,
    seed_win,
    coords_ref,
    counts_ref,
    w1_hbm,
    w2_hbm,
    out_ref,
    grad_ref,
    term1_ref,
    term2_ref,
    win,
    w1,
    w2,
    sems,
):
    loads = [
        pltpu.make_async_copy(w1_hbm, w1, sems.at[0]),
        pltpu.make_async_copy(w2_hbm, w2, sems.at[1]),
    ]
    for load in loads:
        load.start()
    build_windows(
        jnp.concatenate([landed_ref[0], rows_ref[0]], axis=0),
        jnp.concatenate([landed_ref[1], rows_ref[1]], axis=0),
        code_ref,
        coords_ref,
        win,
    )
    live = live_rows(counts_ref)
    feat = jnp.where(live, feat_ref[...].astype(F32), 0.0).T.astype(BF16)
    hidden = rows_ref[0].astype(F32).T.astype(BF16)
    for tap in range(27):
        back = 26 - tap
        place = pl.ds(tap * C, C)
        term1_ref[place, :] = scale * jnp.dot(
            feat, tap_rows(win, 1, back), preferred_element_type=F32
        )
        seed = seed_win[back % 9, :, back // 9 : back // 9 + 4].reshape(ROWS, C)
        term2_ref[place, :] = scale * jnp.dot(hidden, seed, preferred_element_type=F32)
    for load in loads:
        load.wait()
    out_ref[...] = jnp.where(live, conv(win, 0, w2), 0.0)
    grad_ref[...] = jnp.where(live, conv_back(win, 1, w1), 0.0)


def vmem():
    return pl.BlockSpec(memory_space=pltpu.VMEM)


def smem():
    return pl.BlockSpec(memory_space=pltpu.SMEM)


def hbm():
    return pl.BlockSpec(memory_space=pl.ANY)


def reduce_weights(term):
    narrowed = lax.psum_scatter(term, "gx", scatter_dimension=0, tiled=True)
    return lax.psum_scatter(narrowed, "gy", scatter_dimension=1, tiled=True)


def per_device(features, block_coords, block_counts, first_weight, second_weight, cotangent):
    feat = features.reshape(ROWS, C)
    cot = cotangent.reshape(ROWS, C)
    coords = block_coords.reshape(1, SLOTS)
    counts = block_counts.reshape(1, 1)
    pick_np, table_np = face_tables()
    pick = jnp.asarray(pick_np, BF16)
    table = jnp.asarray(table_np)
    struct = jax.ShapeDtypeStruct
    scale = 1.0 / math.sqrt(64 * SLOTS * lax.axis_size("gx") * lax.axis_size("gy"))
    landed, code = pl.pallas_call(
        first_swap_kernel,
        out_shape=(struct((2, FACE, C), BF16), struct((8, DATA), jnp.int32)),
        in_specs=[vmem()] * 4 + [smem()] * 2,
        out_specs=(vmem(), vmem()),
        scratch_shapes=[
            pltpu.VMEM((2, FACE, C), BF16),
            pltpu.VMEM((8, FACE), jnp.int32),
            pltpu.VMEM((2, FACE, C), BF16),
            pltpu.VMEM((8, 8, FACE), jnp.int32),
        ]
        + [pltpu.SemaphoreType.DMA((8,))] * 4,
        compiler_params=pltpu.CompilerParams(collective_id=0, has_side_effects=True),
        name="first_swap",
    )(feat, cot, pick, table, coords, counts)
    weights = [pltpu.VMEM((27 * C, C), BF16)] * 2 + [pltpu.SemaphoreType.DMA((2,))]
    window = (9, SLOTS, 6, 16, C)
    rows, packed, seed_win = pl.pallas_call(
        middle_kernel,
        out_shape=(
            struct((2, ROWS, C), BF16),
            struct((2, FACE, C), BF16),
            struct(window, BF16),
        ),
        in_specs=[vmem()] * 5 + [smem()] * 2 + [hbm()] * 2,
        out_specs=(vmem(), vmem(), vmem()),
        scratch_shapes=[pltpu.VMEM((2,) + window, BF16)] + weights,
        compiler_params=pltpu.CompilerParams(vmem_limit_bytes=40 << 20),
        name="middle",
    )(feat, cot, landed, code, pick, coords, counts, first_weight, second_weight)
    landed2 = pl.pallas_call(
        second_swap_kernel,
        out_shape=struct((2, FACE, C), BF16),
        in_specs=[vmem()],
        out_specs=vmem(),
        scratch_shapes=[pltpu.VMEM((2, FACE, C), BF16)] + [pltpu.SemaphoreType.DMA((8,))] * 2,
        compiler_params=pltpu.CompilerParams(collective_id=1, has_side_effects=True),
        name="second_swap",
    )(packed)
    out, grad, term1, term2 = pl.pallas_call(
        functools.partial(last_kernel, scale),
        out_shape=(
            struct((ROWS, C), F32),
            struct((ROWS, C), F32),
            struct((27 * C, C), F32),
            struct((27 * C, C), F32),
        ),
        in_specs=[vmem()] * 5 + [smem()] * 2 + [hbm()] * 2,
        out_specs=(vmem(),) * 4,
        scratch_shapes=[pltpu.VMEM((2,) + window, BF16)] + weights,
        compiler_params=pltpu.CompilerParams(vmem_limit_bytes=56 << 20),
        name="last",
    )(rows, landed2, code, feat, seed_win, coords, counts, first_weight, second_weight)
    return (
        out.reshape(features.shape),
        grad.reshape(features.shape),
        reduce_weights(term1),
        reduce_weights(term2),
    )


def solution(mesh):
    placed = (
        P("gx", "gy", None, None, None),
        P("gx", "gy", None),
        P("gx", "gy"),
        P(),
        P(),
        P("gx", "gy", None, None, None),
    )
    return jax.shard_map(
        per_device,
        mesh=mesh,
        in_specs=placed,
        out_specs=(
            P("gx", "gy", None, None, None),
            P("gx", "gy", None, None, None),
            P("gx", "gy"),
            P("gx", "gy"),
        ),
        check_vma=False,
    )
```

time: 619 us -> 435 us (0.70)
  the two profiles are of different devices: /device:TPU:32 before, /device:TPU:97 now
where the time goes in v1:
time: 435 us; the launch traced here: 428 us
  waiting for transfers between devices  357 us (82%)
  Pallas kernels  41.7 us (10%)
  local copies, waits for them, and re-layouts  15 us (3%)
  between operations  14.5 us (3%)
    reduce_scatter x2, waiting for transfers between devices, reduce_weights(): narrowed = lax.psum_scatter(term, 'gx', scatter_dimension=0, tiled=True)  276 us
    unnamed x6, waiting for transfers between devices  80.9 us
    unnamed x24, local copies, waits for them, and re-layouts  15 us
    pallas_call x1, Pallas kernels, per_device(): pl.pallas_call(first_swap_kernel, out_shape=(struct((2, FACE, C), BF16),...  12.7 us
    pallas_call x1, Pallas kernels, per_device(): pl.pallas_call(second_swap_kernel, out_shape=struct((2, FACE, C), BF16),...  11.4 us
    pallas_call x1, Pallas kernels, per_device(): pl.pallas_call(functools.partial(last_kernel, scale), out_shape=(struct((...  10.6 us
  transfers between devices with their start and end apart: 4, of which 4 were waited for; matrix products, arithmetic and copies ran while one was open for 1% of the time, Pallas kernels for 0%

profile of v1, /device:TPU:97, one launch (start us, length us, event | category | flops | bytes accessed | tf_op | source)
XLA Modules:
  0.0 428.4 jit_solution(13311011312436794870)
XLA Ops:
  7.9 12.7 %first_swap.1 = (bf16[2,256,256]{2,1,0:T(8,128)(2,1)}, s32[8,448]{1,0:T(8,128)}) custom-call(bf16[192,256]{1,0:T(8,128)(2,1)} %bitcast.9, bf16[192,256]{1,0:T(8,128)(2,1)} %bitcast.12, bf16[256,192]{1,0:T(8,128)(2,1)} %constant.4.clone.pick_ref, s32[8,256]{1,0:T(8,128)} %constant.5.clone.table_ref, s32[1,3]{1,0:T(1,128)} %bitcast.14, s32[1,1]{1,0:T(1,128)S(6)} %copy.20.counts_ref), custom_call_target="tpu_custom_call" | custom-call | tf_op jit(solution)/shard_map/first_swap/pallas_call | solution.py:352
  20.6 2.0 copy-done
  22.6 2.0 copy-done.1
  24.6 0.9 copy-done.3
  25.5 0.9 copy-done.4
  26.4 0.9 copy-done.5
  27.3 0.9 copy-done.6
  28.2 0.7 copy-done.9
  29.0 0.7 copy-done.10
  29.6 7.0 %middle.1 = (bf16[2,192,256]{2,1,0:T(8,128)(2,1)S(1)}, bf16[2,256,256]{2,1,0:T(8,128)(2,1)S(1)}, bf16[9,3,6,16,256]{4,3,2,1,0:T(8,128)(2,1)S(1)}) custom-call(bf16[192,256]{1,0:T(8,128)(2,1)S(1)} %bitcast.11, bf16[192,256]{1,0:T(8,128)(2,1)S(1)} %bitcast.13, bf16[2,256,256]{2,1,0:T(8,128)(2,1)S(1)} %copy-done.6, s32[8,448]{1,0:T(8,128)S(1)} %copy-done.9, ...), custom_call_target="tpu_custom_call" | custom-call | tf_op jit(solution)/shard_map/middle/pallas_call | solution.py:369
  36.6 1.1 copy-done.2
  37.7 0.7 copy-done.7
  38.4 0.7 copy-done.8
  39.0 11.4 %second_swap.1.landed_ref = bf16[2,256,256]{2,1,0:T(8,128)(2,1)} custom-call(bf16[2,256,256]{2,1,0:T(8,128)(2,1)} %copy-done.7), custom_call_target="tpu_custom_call" | custom-call | tf_op jit(solution)/shard_map/second_swap/pallas_call | solution.py:382
  50.4 10.6 %last.1 = (f32[192,256]{1,0:T(8,128)}, f32[192,256]{1,0:T(8,128)}, f32[6912,256]{1,0:T(8,128)}, f32[6912,256]{1,0:T(8,128)}) custom-call(bf16[2,192,256]{2,1,0:T(8,128)(2,1)} %copy-done.8, bf16[2,256,256]{2,1,0:T(8,128)(2,1)} %second_swap.1.landed_ref, s32[8,448]{1,0:T(8,128)} %get-tuple-element.14.code_ref, bf16[192,256]{1,0:T(8,128)(2,1)} %bitcast.10, ...), custom_call_target="tpu_custom_call" | custom-call | tf_op jit(solution)/shard_map/last/pallas_call | solution.py:391
  61.0 0.0 reduce-scatter.9.cloned.1.call-start
  61.1 0.7 reduce-scatter.9.cloned.1.call-update
  61.8 135.6 %reduce-scatter.11.cloned.1.call-done = f32[216,256]{1,0:T(8,128)} async-done(((f32[6912,256]{1,0:T(8,128)}), f32[216,256]{1,0:T(8,128)}) %reduce-scatter.11.cloned.1.call-update) | async-done | bytes 221200 | tf_op jit(solution)/shard_map/reduce_scatter | solution.py:338
  197.5 1.8 copy.18
  199.3 0.0 reduce-scatter.13.cloned.1.call-start
  199.3 140.6 %reduce-scatter.9.cloned.1.call-done = f32[216,256]{1,0:T(8,128)} async-done(((f32[6912,256]{1,0:T(8,128)}), f32[216,256]{1,0:T(8,128)}) %reduce-scatter.9.cloned.1.call-update) | async-done | bytes 221200 | tf_op jit(solution)/shard_map/reduce_scatter | solution.py:338
  339.9 1.8 copy.16
  341.7 38.3 %reduce-scatter.15.cloned.1.call-done = f32[32,216]{1,0:T(8,128)} async-done(((f32[256,216]{1,0:T(8,128)}), f32[32,216]{1,0:T(8,128)}) %reduce-scatter.15.cloned.1.call-update) | async-done | bytes 27664
  380.0 41.8 %reduce-scatter.13.cloned.1.call-done = f32[32,216]{1,0:T(8,128)} async-done(((f32[256,216]{1,0:T(8,128)}), f32[32,216]{1,0:T(8,128)}) %reduce-scatter.13.cloned.1.call-update) | async-done | bytes 27664
  (16 shorter events, 0.1 us)
Async XLA Ops:
  7.2 190.3 %reduce-scatter.11.cloned.1.call-start = ((), (), s32[]{:S(2)}) async-start(), calls=%async_computation.5 | async-start | bytes 7299072 | tf_op jit(solution)/shard_map/reduce_scatter | solution.py:338
  20.6 2.0 copy-start
  22.6 2.0 copy-start.1
  24.6 0.9 copy-start.3
  25.5 0.9 copy-start.4
  26.4 0.9 copy-start.5
  27.3 0.9 copy-start.6
  28.2 0.7 copy-start.9
  29.0 0.7 copy-start.10
  36.6 1.1 copy-start.2
  37.7 0.7 copy-start.7
  38.4 0.7 copy-start.8
  61.0 278.9 %reduce-scatter.9.cloned.1.call-start = ((), (), s32[]{:S(2)}) async-start(), calls=%async_computation.4 | async-start | bytes 7299072 | tf_op jit(solution)/shard_map/reduce_scatter | solution.py:338
  61.8 318.2 %reduce-scatter.15.cloned.1.call-start = ((), (), s32[]{:S(2)}) async-start(), calls=%async_computation.7 | async-start | bytes 294912
  199.3 222.6 %reduce-scatter.13.cloned.1.call-start = ((), (), s32[]{:S(2)}) async-start(), calls=%async_computation.6 | async-start | bytes 294912
Sparse Core Ops, SparseCore 0:
  61.2 136.2 reduce-scatter.10
  201.8 138.0 reduce-scatter.8
  343.0 36.9 reduce-scatter.14
  383.1 38.6 reduce-scatter.12

commit v2 on v1

--- a/solution.py
+++ b/solution.py
@@ -101,14 +101,19 @@
     return copies
 
 
-def greet_around():
+def around():
     nx, ny = lax.axis_size("gx"), lax.axis_size("gy")
     gx, gy = lax.axis_index("gx"), lax.axis_index("gy")
+    return [
+        (lax.rem(gx - sx + nx, nx), lax.rem(gy - sy + ny, ny)) for sx, sy, _, _ in REGIONS
+    ]
+
+
+def greet(peers):
     barrier = pltpu.get_barrier_semaphore()
-    for sx, sy, _, _ in REGIONS:
-        peer = (lax.rem(gx - sx + nx, nx), lax.rem(gy - sy + ny, ny))
+    for peer in peers:
         pl.semaphore_signal(barrier, inc=1, device_id=peer, device_id_type=MESH)
-    pl.semaphore_wait(barrier, 8)
+    pl.semaphore_wait(barrier, len(peers))
 
 
 def first_swap_kernel(
@@ -140,7 +145,7 @@
     inside = (to_x >= 0) & (to_x < nx) & (to_y >= 0) & (to_y < ny)
     sent = table_ref[1:2, :] + by_slot(table_ref[0:1, :], blocks)
     code[...] = jnp.broadcast_to(jnp.where(inside, sent, DEAD), (8, FACE))
-    greet_around()
+    greet(around())
     copies = swap_faces(
         packed, landed, send_sems, recv_sems, ((code, codes_in, code_send, code_recv),)
     )
@@ -158,16 +163,6 @@
     for index in range(1, 8):
         got = jnp.where(region == index, codes_in[index], got)
     code_out[:, :FACE] = got
-
-
-def second_swap_kernel(packed, landed_out, landed, send_sems, recv_sems):
-    greet_around()
-    copies = swap_faces(packed, landed, send_sems, recv_sems)
-    for copy in copies:
-        copy.start()
-    for copy in copies:
-        copy.wait()
-    landed_out[...] = landed[...]
 
 
 def build_windows(first, second, code_ref, coords_ref, win_ref):
@@ -237,7 +232,6 @@
     w2_hbm,
     rows_out,
     packed_out,
-    seed_win_out,
     win,
     w1,
     w2,
@@ -269,24 +263,18 @@
     pick = pick_ref[...]
     packed_out[0] = jnp.dot(pick, hidden, preferred_element_type=F32).astype(BF16)
     packed_out[1] = jnp.dot(pick, pre_grad, preferred_element_type=F32).astype(BF16)
-    seed_win_out[...] = win[1]
 
 
 def last_kernel(
-    scale,
     rows_ref,
     landed_ref,
     code_ref,
-    feat_ref,
-    seed_win,
     coords_ref,
     counts_ref,
     w1_hbm,
     w2_hbm,
     out_ref,
     grad_ref,
-    term1_ref,
-    term2_ref,
     win,
     w1,
     w2,
@@ -306,22 +294,357 @@
         win,
     )
     live = live_rows(counts_ref)
-    feat = jnp.where(live, feat_ref[...].astype(F32), 0.0).T.astype(BF16)
-    hidden = rows_ref[0].astype(F32).T.astype(BF16)
-    for tap in range(27):
-        back = 26 - tap
-        place = pl.ds(tap * C, C)
-        term1_ref[place, :] = scale * jnp.dot(
-            feat, tap_rows(win, 1, back), preferred_element_type=F32
-        )
-        seed = seed_win[back % 9, :, back // 9 : back // 9 + 4].reshape(ROWS, C)
-        term2_ref[place, :] = scale * jnp.dot(hidden, seed, preferred_element_type=F32)
     for load in loads:
         load.wait()
     out_ref[...] = jnp.where(live, conv(win, 0, w2), 0.0)
     grad_ref[...] = jnp.where(live, conv_back(win, 1, w1), 0.0)
 
 
+BLOCK = 216
+TILES = 27
+PACKED = 56
+
+
+class Ring:
+    def __init__(self, own, out, inbox, sends, recvs, me, right, left, place):
+        self.own, self.out, self.inbox = own, out, inbox
+        self.me = place(me)
+        self.to_right = place(lax.rem(me + 1, 4))
+        self.to_left = place(lax.rem(me + 3, 4))
+        across = place(lax.rem(me + 2, 4))
+        self.half = own.shape[1] // 2
+        low, high = pl.ds(0, self.half), pl.ds(self.half, self.half)
+        plan = (
+            (across, high, right),
+            (across, low, left),
+            (self.to_right, low, right),
+            (self.to_left, high, left),
+            (self.to_right, high, right),
+            (self.to_left, low, left),
+        )
+        self.copies = [
+            pltpu.make_async_remote_copy(
+                src_ref=out.at[target, part],
+                dst_ref=inbox.at[index],
+                send_sem=sends.at[index],
+                recv_sem=recvs.at[index],
+                device_id=peer,
+                device_id_type=MESH,
+            )
+            for index, (target, part, peer) in enumerate(plan)
+        ]
+
+    def start(self):
+        for copy in self.copies[:4]:
+            copy.start()
+
+    def relay(self):
+        half = self.half
+        for index, target, base in ((0, self.to_right, half), (1, self.to_left, 0)):
+            self.copies[index].wait_recv()
+
+            @pl.loop(0, half)
+            def _(z):
+                total = self.own[target, base + z] + self.inbox[index, z].astype(F32)
+                self.out[target, base + z] = total.astype(BF16)
+
+            self.copies[4 + index].start()
+
+    def arrive(self):
+        for copy in self.copies[2:]:
+            copy.wait_recv()
+
+    def total(self, z, upper):
+        first, second = (3, 4) if upper else (2, 5)
+        mine = self.own[self.me, z + self.half if upper else z]
+        return mine + self.inbox[first, z].astype(F32) + self.inbox[second, z].astype(F32)
+
+    def drain(self):
+        for copy in self.copies:
+            copy.wait_send()
+
+
+def ring_scratch(nz, rows):
+    return [
+        pltpu.VMEM((4, nz, rows, 128), F32),
+        pltpu.VMEM((4, nz, rows, 128), BF16),
+        pltpu.VMEM((6, nz // 2, rows, 128), BF16),
+        pltpu.SemaphoreType.DMA((6,)),
+        pltpu.SemaphoreType.DMA((6,)),
+    ]
+
+
+def reduce_scratch(nz):
+    return (
+        ring_scratch(nz, BLOCK) * 2
+        + ring_scratch(nz, PACKED) * 2
+        + [
+            pltpu.VMEM((2, nz, PACKED, 128), F32),
+            pltpu.VMEM((2, nz, PACKED, 128), F32),
+            pltpu.VMEM((2, PACKED, 128), F32),
+            pltpu.VMEM((PACKED, 128), F32),
+            pltpu.SemaphoreType.DMA((2, nz)),
+            pltpu.SemaphoreType.DMA((2, nz)),
+            pltpu.SemaphoreType.DMA((2,)),
+        ]
+    )
+
+
+def swapped(t):
+    return lax.rem(t, 2) * 2 + t // 2
+
+
+def straight(t):
+    return t
+
+
+def chip_place():
+    gx, gy = lax.axis_index("gx"), lax.axis_index("gy")
+    z, x, core, y = gx // 4, (lax.rem(gx, 4) // 2) * 2 + lax.rem(gy, 2), lax.rem(gx, 2), gy // 2
+    return x, y, z, core
+
+
+def device_at(x, y, z, core):
+    return (z * 4 + (x // 2) * 2 + core, y * 2 + lax.rem(x, 2))
+
+
+def reduce_peers(nz):
+    x, y, z, core = chip_place()
+    return (
+        [device_at(x, y, z, 1 - core)]
+        + [device_at(lax.rem(x + step, 4), y, z, core) for step in (1, 3)]
+        + [device_at(x, lax.rem(y + step, 4), z, core) for step in (1, 3)]
+        + [device_at(x, y, lax.rem(z + step, nz), core) for step in range(1, nz)]
+    )
+
+
+def spread(rows, own, out, z):
+    lane = lax.broadcasted_iota(jnp.int32, (8, 128), 1) // 32
+    tiles = rows.reshape(TILES, 8, 128)
+    for target in range(4):
+        packed = []
+        for group in range(7):
+            tile = None
+            for part in range(4):
+                index = 4 * group + part
+                if index >= TILES:
+                    continue
+                shift = (part - target) % 4 * 32
+                moved = pltpu.roll(tiles[index], shift, 1) if shift else tiles[index]
+                tile = moved if tile is None else jnp.where(lane == part, moved, tile)
+            packed.append(tile)
+        block = jnp.concatenate(packed, axis=0)
+        own[target, z] = block
+        out[target, z] = block.astype(BF16)
+
+
+def unspread(packed, target_ref):
+    tiles = packed.reshape(7, 8, 128)
+    for index in range(TILES):
+        tile = tiles[index // 4]
+        part = index % 4
+        moved = pltpu.roll(tile, 128 - 32 * part, 1) if part else tile
+        target_ref[index * 8 : index * 8 + 8, :] = moved[:, :32]
+
+
+def reduce_terms(nz, scale, term, first_ref, second_ref, scratch):
+    x, y, z, core = chip_place()
+    xs, ys, ys2, xs2 = (scratch[5 * i : 5 * i + 5] for i in range(4))
+    zown, zin, last, got, zsend, zrecv, psem = scratch[20:]
+    x_right = device_at(lax.rem(x + 1, 4), y, z, core)
+    x_left = device_at(lax.rem(x + 3, 4), y, z, core)
+    y_right = device_at(x, lax.rem(y + 1, 4), z, core)
+    y_left = device_at(x, lax.rem(y + 3, 4), z, core)
+    partner = device_at(x, y, z, 1 - core)
+    firsts = [
+        Ring(*xs, x, x_right, x_left, straight),
+        Ring(*ys, y, y_right, y_left, straight),
+    ]
+    seconds = [
+        Ring(*ys2, y, y_right, y_left, swapped),
+        Ring(*xs2, x, x_right, x_left, straight),
+    ]
+    lane = lax.broadcasted_iota(jnp.int32, (BLOCK, 128), 1)
+    even = (lane // 32) % 2 == 0
+    below = lane < 64
+
+    def place(target, index, value):
+        own, out = target
+        own[index] = value
+        out[index] = value.astype(BF16)
+
+    @pl.loop(0, 2 * nz)
+    def _(block):
+        to_z, to_xh = block // 2, lax.rem(block, 2)
+        rows = pl.ds(pl.multiple_of(block * (2 * BLOCK), 8), BLOCK)
+        left, right = term[rows, :128], term[rows, 128:]
+        place(xs[:2], (2 * to_xh, to_z), jnp.where(even, left, pltpu.roll(right, 32, 1)))
+        place(xs[:2], (2 * to_xh + 1, to_z), jnp.where(even, pltpu.roll(left, 96, 1), right))
+
+    firsts[0].start()
+
+    @pl.loop(0, nz)
+    def _(to_z):
+        rows = [
+            pl.ds(pl.multiple_of(to_z * (4 * BLOCK) + (2 * half + 1) * BLOCK, 8), BLOCK)
+            for half in range(2)
+        ]
+        for pair in range(2):
+            lanes = slice(128 * pair, 128 * pair + 128)
+            zero, one = term[rows[0], lanes], term[rows[1], lanes]
+            place(ys[:2], (2 * pair, to_z), jnp.where(below, zero, pltpu.roll(one, 64, 1)))
+            place(ys[:2], (2 * pair + 1, to_z), jnp.where(below, pltpu.roll(zero, 64, 1), one))
+
+    firsts[1].start()
+    for ring in firsts:
+        ring.relay()
+    for ring, following in zip(firsts, seconds):
+        ring.arrive()
+        half = ring.half
+
+        for upper in range(2):
+
+            @pl.loop(0, half)
+            def _(index):
+                spread(
+                    ring.total(index, upper),
+                    following.own,
+                    following.out,
+                    index + upper * half,
+                )
+
+        following.start()
+    for ring in seconds:
+        ring.relay()
+    zcopies = []
+    for color, ring in enumerate(seconds):
+        ring.arrive()
+        half = ring.half
+
+        for upper in range(2):
+
+            @pl.loop(0, half)
+            def _(index):
+                zown[color, index + upper * half] = ring.total(index, upper)
+
+        for step in range(1, nz):
+            to_z = lax.rem(z + step, nz)
+            copy = pltpu.make_async_remote_copy(
+                src_ref=zown.at[color, to_z],
+                dst_ref=zin.at[color, step],
+                send_sem=zsend.at[color, step],
+                recv_sem=zrecv.at[color, step],
+                device_id=device_at(x, y, to_z, core),
+                device_id_type=MESH,
+            )
+            copy.start()
+            zcopies.append(copy)
+    for color in range(2):
+        total = zown[color, z]
+        for step in range(1, nz):
+            zcopies[color * (nz - 1) + step - 1].wait_recv()
+            total += zin[color, step]
+        last[color] = total * scale
+    copy = pltpu.make_async_remote_copy(
+        src_ref=last.at[1 - core],
+        dst_ref=got,
+        send_sem=psem.at[0],
+        recv_sem=psem.at[1],
+        device_id=partner,
+        device_id_type=MESH,
+    )
+    copy.start()
+    for ring in firsts + seconds:
+        ring.drain()
+    for sent in zcopies:
+        sent.wait_send()
+    copy.wait()
+    mine, other = last[core], got[...]
+    first = core == 0
+    unspread(jnp.where(first, mine, other), first_ref)
+    unspread(jnp.where(first, other, mine), second_ref)
+
+
+def reduce_kernel(
+    nz,
+    scale,
+    win_ref,
+    rows_ref,
+    packed,
+    landed_out,
+    first_ref,
+    second_ref,
+    landed,
+    send_sems,
+    recv_sems,
+    pair_win,
+    pair_rows,
+    pair_sems,
+    turned,
+    term,
+    *scratch,
+):
+    x, y, z, core = chip_place()
+    greet(around() + reduce_peers(nz))
+    partner = device_at(x, y, z, 1 - core)
+    pair = [
+        pltpu.make_async_remote_copy(
+            src_ref=source,
+            dst_ref=target,
+            send_sem=pair_sems.at[2 * index],
+            recv_sem=pair_sems.at[2 * index + 1],
+            device_id=partner,
+            device_id_type=MESH,
+        )
+        for index, (source, target) in enumerate(
+            ((win_ref.at[1 - core], pair_win), (rows_ref.at[core], pair_rows))
+        )
+    ]
+    for copy in pair:
+        copy.start()
+    faces = swap_faces(packed, landed, send_sems, recv_sems)
+    for copy in faces:
+        copy.start()
+    for copy in pair:
+        copy.wait()
+
+    def window(tap):
+        shift, start = lax.rem(tap, 9), tap // 9
+        return jnp.concatenate(
+            [
+                win_ref[core, shift, :, pl.ds(start, 4)].reshape(ROWS, C),
+                pair_win[shift, :, pl.ds(start, 4)].reshape(ROWS, C),
+            ],
+            axis=0,
+        )
+
+    @pl.when(core == 0)
+    def _():
+        right = jnp.concatenate([rows_ref[1], pair_rows[...]], axis=0)
+
+        @pl.loop(0, 27)
+        def _(tap):
+            term[pl.ds(pl.multiple_of(tap * C, C), C), :] = lax.dot_general(
+                window(tap), right, (((0,), (0,)), ((), ())), preferred_element_type=F32
+            )
+
+    @pl.when(core == 1)
+    def _():
+        both = jnp.concatenate([rows_ref[0], pair_rows[...]], axis=0)
+        turned[...] = both.astype(F32).T.astype(BF16)
+
+        @pl.loop(0, 27)
+        def _(tap):
+            term[pl.ds(pl.multiple_of(tap * C, C), C), :] = jnp.dot(
+                turned[...], window(26 - tap), preferred_element_type=F32
+            )
+
+    reduce_terms(nz, scale, term, first_ref, second_ref, scratch)
+    for copy in faces:
+        copy.wait()
+    landed_out[...] = landed[...]
+
+
 def vmem():
     return pl.BlockSpec(memory_space=pltpu.VMEM)
 
@@ -332,11 +655,6 @@
 
 def hbm():
     return pl.BlockSpec(memory_space=pl.ANY)
-
-
-def reduce_weights(term):
-    narrowed = lax.psum_scatter(term, "gx", scatter_dimension=0, tiled=True)
-    return lax.psum_scatter(narrowed, "gy", scatter_dimension=1, tiled=True)
 
 
 def per_device(features, block_coords, block_counts, first_weight, second_weight, cotangent):
@@ -366,48 +684,55 @@
     )(feat, cot, pick, table, coords, counts)
     weights = [pltpu.VMEM((27 * C, C), BF16)] * 2 + [pltpu.SemaphoreType.DMA((2,))]
     window = (9, SLOTS, 6, 16, C)
-    rows, packed, seed_win = pl.pallas_call(
+    rows, packed, win = pl.pallas_call(
         middle_kernel,
         out_shape=(
             struct((2, ROWS, C), BF16),
             struct((2, FACE, C), BF16),
-            struct(window, BF16),
+            struct((2,) + window, BF16),
         ),
         in_specs=[vmem()] * 5 + [smem()] * 2 + [hbm()] * 2,
         out_specs=(vmem(), vmem(), vmem()),
-        scratch_shapes=[pltpu.VMEM((2,) + window, BF16)] + weights,
+        scratch_shapes=weights,
         compiler_params=pltpu.CompilerParams(vmem_limit_bytes=40 << 20),
         name="middle",
     )(feat, cot, landed, code, pick, coords, counts, first_weight, second_weight)
-    landed2 = pl.pallas_call(
-        second_swap_kernel,
-        out_shape=struct((2, FACE, C), BF16),
-        in_specs=[vmem()],
-        out_specs=vmem(),
-        scratch_shapes=[pltpu.VMEM((2, FACE, C), BF16)] + [pltpu.SemaphoreType.DMA((8,))] * 2,
-        compiler_params=pltpu.CompilerParams(collective_id=1, has_side_effects=True),
-        name="second_swap",
-    )(packed)
-    out, grad, term1, term2 = pl.pallas_call(
-        functools.partial(last_kernel, scale),
+    nz = lax.axis_size("gx") // 4
+    landed2, first_grad, second_grad = pl.pallas_call(
+        functools.partial(reduce_kernel, nz, scale),
         out_shape=(
-            struct((ROWS, C), F32),
-            struct((ROWS, C), F32),
-            struct((27 * C, C), F32),
-            struct((27 * C, C), F32),
+            struct((2, FACE, C), BF16),
+            struct((BLOCK, 32), F32),
+            struct((BLOCK, 32), F32),
         ),
-        in_specs=[vmem()] * 5 + [smem()] * 2 + [hbm()] * 2,
-        out_specs=(vmem(),) * 4,
+        in_specs=[vmem()] * 3,
+        out_specs=(vmem(), vmem(), vmem()),
+        scratch_shapes=[
+            pltpu.VMEM((2, FACE, C), BF16),
+            pltpu.SemaphoreType.DMA((8,)),
+            pltpu.SemaphoreType.DMA((8,)),
+            pltpu.VMEM(window, BF16),
+            pltpu.VMEM((ROWS, C), BF16),
+            pltpu.SemaphoreType.DMA((4,)),
+            pltpu.VMEM((C, 2 * ROWS), BF16),
+            pltpu.VMEM((27 * C, C), F32),
+        ]
+        + reduce_scratch(nz),
+        compiler_params=pltpu.CompilerParams(
+            collective_id=1, has_side_effects=True, vmem_limit_bytes=50 << 20
+        ),
+        name="reduce",
+    )(win, rows, packed)
+    out, grad = pl.pallas_call(
+        last_kernel,
+        out_shape=(struct((ROWS, C), F32), struct((ROWS, C), F32)),
+        in_specs=[vmem()] * 3 + [smem()] * 2 + [hbm()] * 2,
+        out_specs=(vmem(), vmem()),
         scratch_shapes=[pltpu.VMEM((2,) + window, BF16)] + weights,
-        compiler_params=pltpu.CompilerParams(vmem_limit_bytes=56 << 20),
+        compiler_params=pltpu.CompilerParams(vmem_limit_bytes=40 << 20),
         name="last",
-    )(rows, landed2, code, feat, seed_win, coords, counts, first_weight, second_weight)
-    return (
-        out.reshape(features.shape),
-        grad.reshape(features.shape),
-        reduce_weights(term1),
-        reduce_weights(term2),
-    )
+    )(rows, landed2, code, coords, counts, first_weight, second_weight)
+    return out.reshape(features.shape), grad.reshape(features.shape), first_grad, second_grad
 
 
 def solution(mesh):

time: 435 us -> 95.8 us (0.22)
  the two profiles are of different devices: /device:TPU:97 before, /device:TPU:1 now
where the time goes in v2:
time: 95.8 us; the launch traced here: 95.4 us
  Pallas kernels  83.7 us (87%)
  local copies, waits for them, and re-layouts  10.4 us (11%)
  between operations  1.36 us (1%)
    pallas_call x1, Pallas kernels, per_device(): pl.pallas_call(functools.partial(reduce_kernel, nz, scale), out_shape=(st...  54 us
    pallas_call x1, Pallas kernels, per_device(): pl.pallas_call(first_swap_kernel, out_shape=(struct((2, FACE, C), BF16),...  17.1 us
    unnamed x26, local copies, waits for them, and re-layouts  10.4 us
    pallas_call x1, Pallas kernels, per_device(): pl.pallas_call(middle_kernel, out_shape=(struct((2, ROWS, C), BF16), stru...  6.84 us
    pallas_call x1, Pallas kernels, per_device(): pl.pallas_call(last_kernel, out_shape=(struct((ROWS, C), F32), struct((RO...  5.75 us

profile of v2, /device:TPU:1, one launch (start us, length us, event | category | flops | bytes accessed | tf_op | source)
XLA Modules:
  0.0 95.4 jit_solution(2005083943853031783)
XLA Ops:
  1.3 17.1 %first_swap.1 = (bf16[2,256,256]{2,1,0:T(8,128)(2,1)}, s32[8,448]{1,0:T(8,128)}) custom-call(bf16[192,256]{1,0:T(8,128)(2,1)} %bitcast.5, bf16[192,256]{1,0:T(8,128)(2,1)} %bitcast.7, bf16[256,192]{1,0:T(8,128)(2,1)} %constant.4.clone.pick_ref, s32[8,256]{1,0:T(8,128)} %constant.5.clone.table_ref, s32[1,3]{1,0:T(1,128)} %bitcast.9, s32[1,1]{1,0:T(1,128)S(6)} %copy.14.counts_ref), custom_call_target="tpu_custom_call" | custom-call | tf_op jit(solution)/shard_map/first_swap/pallas_call | solution.py:670
  18.4 0.0 copy-start
  18.4 2.0 %copy-done = bf16[6912,256]{1,0:T(8,128)(2,1)S(1)} copy-done((bf16[6912,256]{1,0:T(8,128)(2,1)S(1)}, bf16[6912,256]{1,0:T(8,128)(2,1)}, u32[]{:S(2)}) %copy-start) | copy-done | bytes 3538968
  20.4 0.0 copy-start.2
  20.4 2.0 %copy-done.2 = bf16[6912,256]{1,0:T(8,128)(2,1)S(1)} copy-done((bf16[6912,256]{1,0:T(8,128)(2,1)S(1)}, bf16[6912,256]{1,0:T(8,128)(2,1)}, u32[]{:S(2)}) %copy-start.2) | copy-done | bytes 3538968
  22.4 0.0 copy-start.4
  22.4 0.9 copy-done.4
  23.3 0.0 copy-start.5
  23.3 0.9 copy-done.5
  24.2 0.0 copy-start.6
  24.2 0.9 copy-done.6
  25.1 0.0 copy-start.7
  25.1 0.9 copy-done.7
  26.0 0.7 copy-done.8
  26.8 0.7 copy-done.10
  27.4 6.8 %middle.1 = (bf16[2,192,256]{2,1,0:T(8,128)(2,1)S(1)}, bf16[2,256,256]{2,1,0:T(8,128)(2,1)S(1)}, bf16[2,9,3,6,16,256]{5,4,3,2,1,0:T(8,128)(2,1)S(1)}) custom-call(bf16[192,256]{1,0:T(8,128)(2,1)S(1)} %bitcast.6, bf16[192,256]{1,0:T(8,128)(2,1)S(1)} %bitcast.8, bf16[2,256,256]{2,1,0:T(8,128)(2,1)S(1)} %copy-done.7, s32[8,448]{1,0:T(8,128)S(1)} %copy-done.8, ...), custom_call_target="tpu_custom_call" | custom-call | tf_op jit(solution)/shard_map/middle/pallas_call | solution.py:687
  34.3 54.0 %reduce.1 = (bf16[2,256,256]{2,1,0:T(8,128)(2,1)S(1)}, f32[216,32]{1,0:T(8,128)S(1)}, f32[216,32]{1,0:T(8,128)S(1)}) custom-call(bf16[2,9,3,6,16,256]{5,4,3,2,1,0:T(8,128)(2,1)S(1)} %get-tuple-element.17.win_ref, bf16[2,192,256]{2,1,0:T(8,128)(2,1)S(1)} %get-tuple-element.16.rows_ref, bf16[2,256,256]{2,1,0:T(8,128)(2,1)S(1)} %get-tuple-element.18.packed), custom_call_target="tpu_custom_call" | custom-call | tf_op jit(solution)/shard_map/reduce/pallas_call | solution.py:701
  88.3 0.0 copy-done.1
  88.3 0.0 copy-done.3
  88.3 0.0 copy-done.9
  88.3 0.0 copy-done.11
  88.3 5.7 %last.1 = (f32[192,256]{1,0:T(8,128)}, f32[192,256]{1,0:T(8,128)}) custom-call(bf16[2,192,256]{2,1,0:T(8,128)(2,1)S(1)} %get-tuple-element.16.rows_ref, bf16[2,256,256]{2,1,0:T(8,128)(2,1)S(1)} %get-tuple-element.19.landed_ref, s32[8,448]{1,0:T(8,128)S(1)} %copy-done.9, s32[1,3]{1,0:T(1,128)S(1)} %bitcast.11, s32[1,1]{1,0:T(1,128)S(6)} %copy.14.counts_ref, ...), custom_call_target="tpu_custom_call" | custom-call | tf_op jit(solution)/shard_map/last/pallas_call | solution.py:726
  94.1 0.7 copy.12
  94.8 0.7 copy.13
  (6 shorter events, 0.0 us)
Async XLA Ops:
  18.4 2.0 %copy-start = (bf16[6912,256]{1,0:T(8,128)(2,1)S(1)}, bf16[6912,256]{1,0:T(8,128)(2,1)}, u32[]{:S(2)}) copy-start(bf16[6912,256]{1,0:T(8,128)(2,1)} %w1_hbm.3) | copy-start | bytes 10616836
  20.4 2.0 %copy-start.2 = (bf16[6912,256]{1,0:T(8,128)(2,1)S(1)}, bf16[6912,256]{1,0:T(8,128)(2,1)}, u32[]{:S(2)}) copy-start(bf16[6912,256]{1,0:T(8,128)(2,1)} %w2_hbm.3) | copy-start | bytes 10616836
  22.4 0.9 copy-start.4
  23.3 0.9 copy-start.5
  24.2 0.9 copy-start.6
  25.1 0.9 copy-start.7
  26.0 0.7 copy-start.8
  26.8 0.7 copy-start.10
  27.4 60.9 %copy-start.1 = (bf16[6912,256]{1,0:T(8,128)(2,1)S(1)}, bf16[6912,256]{1,0:T(8,128)(2,1)}, u32[]{:S(2)}) copy-start(bf16[6912,256]{1,0:T(8,128)(2,1)} %w1_hbm.3) | copy-start | bytes 10616836
  27.4 60.9 %copy-start.3 = (bf16[6912,256]{1,0:T(8,128)(2,1)S(1)}, bf16[6912,256]{1,0:T(8,128)(2,1)}, u32[]{:S(2)}) copy-start(bf16[6912,256]{1,0:T(8,128)(2,1)} %w2_hbm.3) | copy-start | bytes 10616836
  27.4 60.9 %copy-start.9 = (s32[8,448]{1,0:T(8,128)S(1)}, s32[8,448]{1,0:T(8,128)}, u32[]{:S(2)}) copy-start(s32[8,448]{1,0:T(8,128)} %get-tuple-element.15.code_ref) | copy-start | bytes 43012
  27.4 60.9 %copy-start.11 = (s32[1,1,3]{2,1,0:T(1,128)S(1)}, s32[1,1,3]{2,1,0:T(1,128)}, u32[]{:S(2)}) copy-start(s32[1,1,3]{2,1,0:T(1,128)} %param.9) | copy-start | bytes 40
